TPU v7x, 512 devices: a whole 4x8x8 slice. The times are simulated.
512 devices in a mesh: dp: 16 (over x_lo, z), fsdp: 32 (over x_hi, y, core).
Axes of the slice: x: 4 (x_hi: 2, x_lo: 2; x = x_hi * 2 + x_lo), y: 8, z: 8, core: 2. Of those that a mesh axis runs over, the one named last changes fastest.
Arguments:
- layer_input: bfloat16 [32768, 8192], P('dp', 'fsdp'), may hold values from -6 to 6
- cotangent: bfloat16 [2, 32768, 1024], P(None, ('dp', 'fsdp')), may hold values from -6 to 6
- candidates: bfloat16 [2, 16, 1024, 512], P(None, 'dp', None, 'fsdp'), may hold values from -0.1875 to 0.1875
- moment_first: float32 [2, 512, 8192], P(None, 'dp', 'fsdp'), may hold values from -0.6 to 0.6
- moment_second: float32 [2, 512, 8192], P(None, 'dp', 'fsdp'), may hold values from 0.0001 to 0.01
- owners: int32 [2], replicated, may hold values from 0 to 15
Outputs:
- update: bfloat16 [2, 1024, 8192], P(None, 'dp', 'fsdp')
- first_next: float32 [2, 512, 8192], P(None, 'dp', 'fsdp')
- second_next: float32 [2, 512, 8192], P(None, 'dp', 'fsdp')
Inputs may be any that keep to these rules, and one draw needn't show every extreme that they name: owners[m] names a data-parallel replica.
All inputs are finite; a program needn't handle non-finite values.
Results may differ from a plain program's by a relative error of at most 0.0056.
Values may be sent and summed in bfloat16 or wider, within the bound.
A program may use at most 64 MiB of HBM per device.

v0:
```python
import math
import jax
import jax.numpy as jnp
from jax import lax
from jax.sharding import PartitionSpec as P

MATS = 2
STEP = 10
beta_first = 0.9
beta_second = 0.999
epsilon = 1e-08


def broadcast(x, axis, root):
    return lax.dynamic_index_in_dim(lax.all_gather(x, axis), root, 0, keepdims=False)


def sent_to_all(x, axis):
    count = lax.axis_size(axis)
    return lax.all_to_all(jnp.broadcast_to(x[None], (count, *x.shape)), axis, 0, 0, tiled=True)


def in_order(blocks, dim):
    lengths = list(blocks.shape[1:])
    lengths[dim] *= blocks.shape[0]
    return jnp.moveaxis(blocks, 0, dim).reshape(lengths)


def collect(x, axis, dim):
    blocks = sent_to_all(x, axis)
    return in_order(blocks, dim)


def cut_along(x, dim, count):
    before, after = (x.shape[:dim], x.shape[dim + 1 :])
    return jnp.moveaxis(x.reshape(*before, count, -1, *after), dim, 0)


def summed_on_arrival(x, axis, dim):
    blocks = cut_along(x, dim, lax.axis_size(axis))
    arrived = lax.all_to_all(blocks, axis, split_axis=0, concat_axis=0, tiled=True)
    return arrived.sum(axis=0)


def on_device(layer_input, cotangent, candidates, moment_first, moment_second, owners):
    replicas = lax.axis_size("dp")
    replica_index = lax.axis_index("dp")
    inverse_root = 1.0 / math.sqrt(layer_input.shape[0] * replicas)
    kv_share = candidates.shape[2] // replicas
    updates = []
    firsts = []
    seconds = []
    for matrix in range(MATS):
        candidate_own = candidates[matrix, 0]
        owner_index = owners[matrix]
        owner_block = broadcast(candidate_own, "dp", owner_index)
        projector = collect(owner_block, "fsdp", 1)
        head_rows = jnp.dot(
            cotangent[matrix], projector, preferred_element_type=jnp.float32
        ).astype(jnp.bfloat16)
        partial_value = lax.dot_general(
            lax.all_gather(head_rows, "fsdp", axis=0, tiled=True),
            layer_input,
            (((0,), (0,)), ((), ())),
            preferred_element_type=jnp.float32,
        )
        projected = summed_on_arrival(partial_value, "dp", 0) * inverse_root
        first = beta_first * moment_first[matrix] + (1.0 - beta_first) * projected
        second = beta_second * moment_second[matrix] + (1.0 - beta_second) * projected * projected
        direction = (
            first
            / (1.0 - beta_first**STEP)
            / (jnp.sqrt(second / (1.0 - beta_second**STEP)) + epsilon)
        )
        direction = direction.astype(jnp.bfloat16)
        own_rows = lax.dynamic_slice_in_dim(projector, replica_index * kv_share, kv_share, 0)
        update = jnp.dot(own_rows, collect(direction, "dp", 0), preferred_element_type=jnp.float32)
        updates.append(update.astype(jnp.bfloat16))
        firsts.append(first)
        seconds.append(second)
    return (jnp.stack(updates), jnp.stack(firsts), jnp.stack(seconds))


def solution(mesh):
    placed = (
        P("dp", "fsdp"),
        P(None, ("dp", "fsdp"), None),
        P(None, "dp", None, "fsdp"),
        P(None, "dp", "fsdp"),
        P(None, "dp", "fsdp"),
        P(),
    )
    return jax.shard_map(
        on_device,
        mesh=mesh,
        in_specs=placed,
        out_specs=(P(None, "dp", "fsdp"), P(None, "dp", "fsdp"), P(None, "dp", "fsdp")),
        check_vma=False,
    )
```

profile of v0, /device:TPU:2, one launch (start us, length us, event | category | flops | bytes accessed | tf_op | source)
XLA Modules:
  0.0 325.7 jit_solution(12973515239512783485)
XLA Ops:
  7.2 0.0 copy-start
  7.2 0.0 copy-start.1
  7.2 0.0 all-gather.7.cloned.1.call-start
  7.2 1.4 fusion.15
  9.9 0.8 fusion.14
  10.7 41.3 %all-gather.1 = bf16[16,1,1024,16]{2,3,1,0:T(8,128)(2,1)S(1)} all-gather(bf16[1,1,1024,16]{2,3,1,0:T(8,128)(2,1)S(1)} %get-tuple-element.13), channel_id=3, replica_groups=mesh['dp'=16,'fsdp'=32] {'dp'}, dimensions={0}, use_global_device_ids=true | all-gather | bytes 557056 | tf_op jit(solution)/shard_map/all_gather | solution.py:15
  52.6 0.1 broadcast_in_dim.37
  52.8 39.1 %all_to_all.30 = bf16[32,1024,16]{1,2,0:T(8,128)(2,1)S(1)} all-to-all(bf16[32,1024,16]{1,2,0:T(8,128)(2,1)S(1)} %broadcast_in_dim.37), channel_id=1, replica_groups=mesh['dp'=16,'fsdp'=32] {'fsdp'}, dimensions={0} | all-to-all | bytes 2097152 | tf_op jit(solution)/shard_map/all_to_all | solution.py:20
  91.9 0.0 copy-done.1
  91.9 1.1 fusion.1
  93.0 0.0 all-gather.7.cloned.1.call-update
  93.0 0.0 all-gather.5.cloned.1.call-start
  95.0 33.0 %all-gather = bf16[16,1,1024,16]{2,3,1,0:T(8,128)(2,1)S(1)} all-gather(bf16[1,1,1024,16]{2,3,1,0:T(8,128)(2,1)S(1)} %get-tuple-element.12), channel_id=2, replica_groups=mesh['dp'=16,'fsdp'=32] {'dp'}, dimensions={0}, use_global_device_ids=true | all-gather | bytes 557056 | tf_op jit(solution)/shard_map/all_gather | solution.py:15
  128.0 0.1 broadcast_in_dim.33
  128.1 37.3 %all_to_all.31 = bf16[32,1024,16]{1,2,0:T(8,128)(2,1)S(1)} all-to-all(bf16[32,1024,16]{1,2,0:T(8,128)(2,1)S(1)} %broadcast_in_dim.33), channel_id=1, replica_groups=mesh['dp'=16,'fsdp'=32] {'fsdp'}, dimensions={0} | all-to-all | bytes 2097152 | tf_op jit(solution)/shard_map/all_to_all | solution.py:20
  165.4 1.1 fusion
  166.5 0.0 all-gather.5.cloned.1.call-update
  166.5 7.0 %all-gather.7.cloned.1.call-done = bf16[2048,512]{1,0:T(8,128)(2,1)} async-done(((bf16[64,512]{1,0:T(8,128)(2,1)}), bf16[2048,512]{1,0:T(8,128)(2,1)}) %all-gather.7.cloned.1.call-update) | async-done | bytes 2097168 | tf_op jit(solution)/shard_map/all_gather | solution.py:62
  173.5 0.0 copy-done
  173.5 3.1 fusion.17
  176.6 7.5 %all-to-all-start.4 = ((f32[16,32,256]{2,1,0:T(8,128)}), f32[16,32,256]{2,1,0:T(8,128)}, u32[]{:S(2)}, u32[]{:S(2)}) async-start(f32[16,32,256]{2,1,0:T(8,128)} %bitcast.59), calls=%async_computation.4 | async-start | bytes 1048576 | tf_op jit(solution)/shard_map/all_to_all | solution.py:41
  184.2 0.0 copy-start.2
  184.2 0.0 copy-start.3
  184.2 75.2 %all-gather.5.cloned.1.call-done = bf16[2048,512]{1,0:T(8,128)(2,1)} async-done(((bf16[64,512]{1,0:T(8,128)(2,1)}), bf16[2048,512]{1,0:T(8,128)(2,1)}) %all-gather.5.cloned.1.call-update) | async-done | bytes 2097168 | tf_op jit(solution)/shard_map/all_gather | solution.py:62
  259.4 3.1 fusion.16
  262.6 0.0 all-to-all-done.4
  262.6 8.9 %all-to-all-start.1 = ((f32[16,32,256]{2,1,0:T(8,128)}), f32[16,32,256]{2,1,0:T(8,128)}, u32[]{:S(2)}, u32[]{:S(2)}) async-start(f32[16,32,256]{2,1,0:T(8,128)} %bitcast.58), calls=%async_computation.1 | async-start | bytes 1048576 | tf_op jit(solution)/shard_map/all_to_all | solution.py:41
  271.4 1.1 reduce_sum.19
  272.5 13.9 %all-to-all-done.1 = f32[16,32,256]{2,1,0:T(8,128)} async-done(((f32[16,32,256]{2,1,0:T(8,128)}), f32[16,32,256]{2,1,0:T(8,128)}, u32[]{:S(2)}, u32[]{:S(2)}) %all-to-all-start.1) | async-done | bytes 524320 | tf_op jit(solution)/shard_map/all_to_all | solution.py:41
  286.4 1.1 reduce_sum.18
  287.5 0.0 copy-done.2
  287.5 0.0 copy-done.3
  287.5 0.1 fusion.10
  287.6 15.1 %all_to_all.32 = bf16[16,32,256]{2,1,0:T(8,128)(2,1)} all-to-all(bf16[16,32,256]{2,1,0:T(8,128)(2,1)S(1)} %broadcast_in_dim.35), channel_id=1, replica_groups=mesh['dp'=16,'fsdp'=32] {'dp'}, dimensions={0} | all-to-all | bytes 524288 | tf_op jit(solution)/shard_map/all_to_all | solution.py:20
  302.8 0.7 broadcast_in_dim.39
  303.5 5.3 %all-to-all-start.5 = ((bf16[16,32,256]{2,1,0:T(8,128)(2,1)}), bf16[16,32,256]{2,1,0:T(8,128)(2,1)S(1)}, u32[]{:S(2)}, u32[]{:S(2)}) async-start(bf16[16,32,256]{2,1,0:T(8,128)(2,1)} %broadcast_in_dim.39), calls=%async_computation.5 | async-start | bytes 524288 | tf_op jit(solution)/shard_map/all_to_all | solution.py:20
  308.8 0.7 pad_maximum_fusion.1
  309.4 1.2 fusion.2
  310.7 7.3 %all-to-all-done.5 = bf16[16,32,256]{2,1,0:T(8,128)(2,1)S(1)} async-done(((bf16[16,32,256]{2,1,0:T(8,128)(2,1)}), bf16[16,32,256]{2,1,0:T(8,128)(2,1)S(1)}, u32[]{:S(2)}, u32[]{:S(2)}) %all-to-all-start.5) | async-done | bytes 262176 | tf_op jit(solution)/shard_map/all_to_all | solution.py:20
  317.9 0.3 fusion.3
  318.2 0.6 pad_maximum_fusion
  (3 shorter events, 0.0 us)
Async XLA Ops:
  7.2 166.3 %copy-start = (bf16[2048,256]{1,0:T(8,128)(2,1)S(1)}, bf16[2048,256]{1,0:T(8,128)(2,1)}, u32[]{:S(2)}) copy-start(bf16[2048,256]{1,0:T(8,128)(2,1)} %param.6) | copy-start | bytes 3145732
  7.2 84.7 %copy-start.1 = (bf16[2,64,1024]{2,1,0:T(8,128)(2,1)S(1)}, bf16[2,64,1024]{2,1,0:T(8,128)(2,1)}, u32[]{:S(2)}) copy-start(bf16[2,64,1024]{2,1,0:T(8,128)(2,1)} %param.7) | copy-start | bytes 786436
  7.2 166.3 %all-gather.7.cloned.1.call-start = ((), (), s32[]{:S(2)}) async-start(), calls=%async_computation.7 | async-start | bytes 2162688 | tf_op jit(solution)/shard_map/all_gather | solution.py:62
  93.0 166.4 %all-gather.5.cloned.1.call-start = ((), (), s32[]{:S(2)}) async-start(), calls=%async_computation.6 | async-start | bytes 2162688 | tf_op jit(solution)/shard_map/all_gather | solution.py:62
  176.6 85.9 %all-to-all-start.4 = ((f32[16,32,256]{2,1,0:T(8,128)}), f32[16,32,256]{2,1,0:T(8,128)}, u32[]{:S(2)}, u32[]{:S(2)}) async-start(f32[16,32,256]{2,1,0:T(8,128)} %bitcast.59), calls=%async_computation.4 | async-start | bytes 1048576 | tf_op jit(solution)/shard_map/all_to_all | solution.py:41
  184.2 103.3 %copy-start.2 = (f32[2,32,256]{2,1,0:T(8,128)S(1)}, f32[2,32,256]{2,1,0:T(8,128)}, u32[]{:S(2)}) copy-start(f32[2,32,256]{2,1,0:T(8,128)} %param.9) | copy-start | bytes 196612
  184.2 103.3 %copy-start.3 = (f32[2,32,256]{2,1,0:T(8,128)S(1)}, f32[2,32,256]{2,1,0:T(8,128)}, u32[]{:S(2)}) copy-start(f32[2,32,256]{2,1,0:T(8,128)} %param.10) | copy-start | bytes 196612
  262.6 23.9 %all-to-all-start.1 = ((f32[16,32,256]{2,1,0:T(8,128)}), f32[16,32,256]{2,1,0:T(8,128)}, u32[]{:S(2)}, u32[]{:S(2)}) async-start(f32[16,32,256]{2,1,0:T(8,128)} %bitcast.58), calls=%async_computation.1 | async-start | bytes 1048576 | tf_op jit(solution)/shard_map/all_to_all | solution.py:41
  303.5 14.5 %all-to-all-start.5 = ((bf16[16,32,256]{2,1,0:T(8,128)(2,1)}), bf16[16,32,256]{2,1,0:T(8,128)(2,1)S(1)}, u32[]{:S(2)}, u32[]{:S(2)}) async-start(bf16[16,32,256]{2,1,0:T(8,128)(2,1)} %broadcast_in_dim.39), calls=%async_computation.5 | async-start | bytes 524288 | tf_op jit(solution)/shard_map/all_to_all | solution.py:20
Sparse Core Ops, SparseCore 0:
  93.1 80.3 all-gather.6
  177.4 81.9 all-gather.4
where the time goes:
time: 327 us; the launch traced here: 326 us
  blocking collectives  166 us (51%)
  waiting for transfers between devices  103 us (31%)
  starting transfers between devices  21.8 us (7%)
  between operations  18 us (6%)
  matrix products  9.98 us (3%)
  other arithmetic  3.52 us (1%)
    all_to_all x3, blocking collectives, sent_to_all(): lax.all_to_all(jnp.broadcast_to(x[None], (count, *x.shape)), axis, 0, 0,...  91.5 us
    all_gather x2, waiting for transfers between devices, on_device(): lax.all_gather(head_rows, 'fsdp', axis=0, tiled=True)  82.2 us
    all_gather x2, blocking collectives, broadcast(): lax.all_gather(x, axis)  74.3 us
    all_to_all x2, starting transfers between devices, summed_on_arrival(): lax.all_to_all(blocks, axis, split_axis=0, concat_axis=0, tiled=True)  16.4 us
    all_to_all x2, waiting for transfers between devices, summed_on_arrival(): lax.all_to_all(blocks, axis, split_axis=0, concat_axis=0, tiled=True)  14 us
    all_to_all x1, waiting for transfers between devices, sent_to_all(): lax.all_to_all(jnp.broadcast_to(x[None], (count, *x.shape)), axis, 0, 0,...  7.26 us
  transfers between devices with their start and end apart: 5, of which 4 were waited for; matrix products, arithmetic and copies ran while one was open for 3% of the time, Pallas kernels for 0%

commit v1 on v0

--- a/solution.py
+++ b/solution.py
@@ -1,3 +1,4 @@
+import functools
 import math
 import jax
 import jax.numpy as jnp
@@ -9,6 +10,21 @@
 beta_first = 0.9
 beta_second = 0.999
 epsilon = 1e-08
+
+
+def fit_scales(q_in, dev_axis, dim_k):
+    return jnp.concatenate(
+        lax.all_to_all(
+            jnp.stack([q_in for _ in range(lax.axis_size(dev_axis))], axis=0),
+            split_axis=0,
+            concat_axis=0,
+            axis_name=dev_axis,
+        ),
+        axis=dim_k,
+    )
+
+
+meet_node_now = functools.partial(fit_scales, dev_axis="fsdp", dim_k=0)
 
 
 def broadcast(x, axis, root):
@@ -59,7 +75,7 @@
             cotangent[matrix], projector, preferred_element_type=jnp.float32
         ).astype(jnp.bfloat16)
         partial_value = lax.dot_general(
-            lax.all_gather(head_rows, "fsdp", axis=0, tiled=True),
+            meet_node_now(head_rows),
             layer_input,
             (((0,), (0,)), ((), ())),
             preferred_element_type=jnp.float32,

time: 327 us -> 322 us (0.985)
  the two profiles are of different devices: /device:TPU:2 before, /device:TPU:8 now
where the time goes in v1:
time: 322 us; the launch traced here: 321 us
  waiting for transfers between devices  158 us (49%)
  blocking collectives  90.1 us (28%)
  starting transfers between devices  39.7 us (12%)
  local copies, waits for them, and re-layouts  15.3 us (5%)
  matrix products  10.7 us (3%)
  between operations  4.73 us (1%)
    all_to_all x2, waiting for transfers between devices, fit_scales(): lax.all_to_all(jnp.stack([q_in for _ in range(lax.axis_size(dev_axis))],...  96.5 us
    all_gather x2, blocking collectives, broadcast(): lax.all_gather(x, axis)  76.2 us
    all_to_all x3, waiting for transfers between devices, sent_to_all(): lax.all_to_all(jnp.broadcast_to(x[None], (count, *x.shape)), axis, 0, 0,...  37.3 us
    all_to_all x2, waiting for transfers between devices, summed_on_arrival(): lax.all_to_all(blocks, axis, split_axis=0, concat_axis=0, tiled=True)  23.9 us
    all_to_all x3, starting transfers between devices, sent_to_all(): lax.all_to_all(jnp.broadcast_to(x[None], (count, *x.shape)), axis, 0, 0,...  23.4 us
    all_to_all x1, blocking collectives, sent_to_all(): lax.all_to_all(jnp.broadcast_to(x[None], (count, *x.shape)), axis, 0, 0,...  14 us
    all_to_all x2, starting transfers between devices, summed_on_arrival(): lax.all_to_all(blocks, axis, split_axis=0, concat_axis=0, tiled=True)  8.76 us
    all_to_all x2, starting transfers between devices, fit_scales(): lax.all_to_all(jnp.stack([q_in for _ in range(lax.axis_size(dev_axis))],...  7.6 us
  transfers between devices with their start and end apart: 7, of which 6 were waited for; matrix products, arithmetic and copies ran while one was open for 6% of the time, Pallas kernels for 0%

profile of v1, /device:TPU:8, one launch (start us, length us, event | category | flops | bytes accessed | tf_op | source)
XLA Modules:
  0.0 320.9 jit_solution(16991067721166193075)
XLA Ops:
  0.6 0.0 copy-start
  0.6 1.3 fusion.19
  3.3 0.8 fusion.18
  4.1 42.3 %all-gather.1 = bf16[16,1,1024,16]{2,3,1,0:T(8,128)(2,1)S(1)} all-gather(bf16[1,1,1024,16]{2,3,1,0:T(8,128)(2,1)S(1)} %get-tuple-element.13), channel_id=3, replica_groups=mesh['dp'=16,'fsdp'=32] {'dp'}, dimensions={0}, use_global_device_ids=true | all-gather | bytes 557056 | tf_op jit(solution)/shard_map/all_gather | solution.py:31
  47.0 1.1 broadcast_in_dim.37
  48.1 9.9 %all-to-all-start.4 = ((bf16[32,1024,16]{1,2,0:T(8,128)(2,1)}), bf16[32,1024,16]{1,2,0:T(8,128)(2,1)S(1)}, u32[]{:S(2)}, u32[]{:S(2)}) async-start(bf16[32,1024,16]{1,2,0:T(8,128)(2,1)} %broadcast_in_dim.37), calls=%async_computation.4 | async-start | bytes 2097152 | tf_op jit(solution)/shard_map/all_to_all | solution.py:36
  58.0 0.0 copy-start.4
  60.0 33.9 %all-gather = bf16[16,1,1024,16]{2,3,1,0:T(8,128)(2,1)S(1)} all-gather(bf16[1,1,1024,16]{2,3,1,0:T(8,128)(2,1)S(1)} %get-tuple-element.12), channel_id=2, replica_groups=mesh['dp'=16,'fsdp'=32] {'dp'}, dimensions={0}, use_global_device_ids=true | all-gather | bytes 557056 | tf_op jit(solution)/shard_map/all_gather | solution.py:31
  93.9 0.0 all-to-all-done.4
  93.9 0.0 copy-start.2
  93.9 1.3 broadcast_in_dim.33
  95.2 9.2 %all-to-all-start = ((bf16[32,1024,16]{1,2,0:T(8,128)(2,1)}), bf16[32,1024,16]{1,2,0:T(8,128)(2,1)S(1)}, u32[]{:S(2)}, u32[]{:S(2)}) async-start(bf16[32,1024,16]{1,2,0:T(8,128)(2,1)} %broadcast_in_dim.33), calls=%async_computation | async-start | bytes 2097152 | tf_op jit(solution)/shard_map/all_to_all | solution.py:36
  104.4 0.0 copy-done.4
  104.4 0.4 fusion.1
  104.8 0.0 copy-done.2
  104.8 30.0 %all-to-all-done = bf16[32,1024,16]{1,2,0:T(8,128)(2,1)S(1)} async-done(((bf16[32,1024,16]{1,2,0:T(8,128)(2,1)}), bf16[32,1024,16]{1,2,0:T(8,128)(2,1)S(1)}, u32[]{:S(2)}, u32[]{:S(2)}) %all-to-all-start) | async-done | bytes 1048608 | tf_op jit(solution)/shard_map/all_to_all | solution.py:36
  134.8 0.0 copy-start.3
  134.8 1.7 stack.16
  136.5 0.0 copy-done.3
  136.5 3.8 %all-to-all-start.5 = ((bf16[32,64,512]{2,1,0:T(8,128)(2,1)}), bf16[32,64,512]{2,1,0:T(8,128)(2,1)S(1)}, u32[]{:S(2)}, u32[]{:S(2)}) async-start(bf16[32,64,512]{2,1,0:T(8,128)(2,1)} %stack.16), calls=%async_computation.5 | async-start | bytes 4194304 | tf_op jit(solution)/shard_map/all_to_all | solution.py:17
  140.3 1.7 fusion
  142.0 51.0 %all-to-all-done.5 = bf16[32,64,512]{2,1,0:T(8,128)(2,1)S(1)} async-done(((bf16[32,64,512]{2,1,0:T(8,128)(2,1)}), bf16[32,64,512]{2,1,0:T(8,128)(2,1)S(1)}, u32[]{:S(2)}, u32[]{:S(2)}) %all-to-all-start.5) | async-done | bytes 2097184 | tf_op jit(solution)/shard_map/all_to_all | solution.py:17
  193.0 0.0 copy-start.1
  193.0 1.7 stack.14
  194.7 0.2 copy-done.1
  194.9 3.8 %all-to-all-start.1 = ((bf16[32,64,512]{2,1,0:T(8,128)(2,1)}), bf16[32,64,512]{2,1,0:T(8,128)(2,1)S(1)}, u32[]{:S(2)}, u32[]{:S(2)}) async-start(bf16[32,64,512]{2,1,0:T(8,128)(2,1)} %stack.14), calls=%async_computation.1 | async-start | bytes 4194304 | tf_op jit(solution)/shard_map/all_to_all | solution.py:17
  198.8 4.0 %copy.14 = bf16[512,2048]{1,0:T(8,128)(2,1)} copy(bf16[512,2048]{0,1:T(8,128)(2,1)} %bitcast.64) | data formatting | bytes 4194304 | tf_op jit(solution)/shard_map/dot_general | solution.py:77
  202.7 0.0 copy-done
  202.7 3.1 fusion.4
  205.8 45.5 %all-to-all-done.1 = bf16[32,64,512]{2,1,0:T(8,128)(2,1)S(1)} async-done(((bf16[32,64,512]{2,1,0:T(8,128)(2,1)}), bf16[32,64,512]{2,1,0:T(8,128)(2,1)S(1)}, u32[]{:S(2)}, u32[]{:S(2)}) %all-to-all-start.1) | async-done | bytes 2097184 | tf_op jit(solution)/shard_map/all_to_all | solution.py:17
  251.4 4.2 %all-to-all-start.6 = ((f32[16,32,256]{2,1,0:T(8,128)}), f32[16,32,256]{2,1,0:T(8,128)}, u32[]{:S(2)}, u32[]{:S(2)}) async-start(f32[16,32,256]{2,1,0:T(8,128)} %fusion.4), calls=%async_computation.6 | async-start | bytes 1048576 | tf_op jit(solution)/shard_map/all_to_all | solution.py:57
  255.6 2.5 copy.13
  258.1 0.0 copy-start.5
  258.1 0.0 copy-start.6
  258.1 3.1 fusion.6
  261.2 10.1 %all-to-all-done.6 = f32[16,32,256]{2,1,0:T(8,128)} async-done(((f32[16,32,256]{2,1,0:T(8,128)}), f32[16,32,256]{2,1,0:T(8,128)}, u32[]{:S(2)}, u32[]{:S(2)}) %all-to-all-start.6) | async-done | bytes 524320 | tf_op jit(solution)/shard_map/all_to_all | solution.py:57
  271.3 4.5 %all-to-all-start.2 = ((f32[16,32,256]{2,1,0:T(8,128)}), f32[16,32,256]{2,1,0:T(8,128)S(1)}, u32[]{:S(2)}, u32[]{:S(2)}) async-start(f32[16,32,256]{2,1,0:T(8,128)} %fusion.6), calls=%async_computation.2 | async-start | bytes 1048576 | tf_op jit(solution)/shard_map/all_to_all | solution.py:57
  275.8 1.1 reduce_sum.19
  276.9 13.8 %all-to-all-done.2 = f32[16,32,256]{2,1,0:T(8,128)S(1)} async-done(((f32[16,32,256]{2,1,0:T(8,128)}), f32[16,32,256]{2,1,0:T(8,128)S(1)}, u32[]{:S(2)}, u32[]{:S(2)}) %all-to-all-start.2) | async-done | bytes 524320 | tf_op jit(solution)/shard_map/all_to_all | solution.py:57
  290.8 0.0 copy-done.5
  290.8 0.0 copy-done.6
  290.8 0.1 fusion.14
  290.9 14.0 %all_to_all.40 = bf16[16,32,256]{2,1,0:T(8,128)(2,1)S(1)} all-to-all(bf16[16,32,256]{2,1,0:T(8,128)(2,1)S(1)} %broadcast_in_dim.35), channel_id=1, replica_groups=mesh['dp'=16,'fsdp'=32] {'dp'}, dimensions={0} | all-to-all | bytes 524288 | tf_op jit(solution)/shard_map/all_to_all | solution.py:36
  304.9 0.7 broadcast_in_dim.39
  305.6 4.3 %all-to-all-start.7 = ((bf16[16,32,256]{2,1,0:T(8,128)(2,1)}), bf16[16,32,256]{2,1,0:T(8,128)(2,1)S(1)}, u32[]{:S(2)}, u32[]{:S(2)}) async-start(bf16[16,32,256]{2,1,0:T(8,128)(2,1)} %broadcast_in_dim.39), calls=%async_computation.7 | async-start | bytes 524288 | tf_op jit(solution)/shard_map/all_to_all | solution.py:36
  309.9 0.7 pad_maximum_fusion.1
  310.6 1.2 fusion.2
  311.7 7.3 %all-to-all-done.7 = bf16[16,32,256]{2,1,0:T(8,128)(2,1)S(1)} async-done(((bf16[16,32,256]{2,1,0:T(8,128)(2,1)}), bf16[16,32,256]{2,1,0:T(8,128)(2,1)S(1)}, u32[]{:S(2)}, u32[]{:S(2)}) %all-to-all-start.7) | async-done | bytes 262176 | tf_op jit(solution)/shard_map/all_to_all | solution.py:36
  319.0 1.2 fusion.3
  320.2 0.6 pad_maximum_fusion
  (4 shorter events, 0.1 us)
Async XLA Ops:
  0.6 202.1 %copy-start = (bf16[2048,256]{1,0:T(8,128)(2,1)S(1)}, bf16[2048,256]{1,0:T(8,128)(2,1)}, u32[]{:S(2)}) copy-start(bf16[2048,256]{1,0:T(8,128)(2,1)} %param.6) | copy-start | bytes 3145732
  48.1 45.8 %all-to-all-start.4 = ((bf16[32,1024,16]{1,2,0:T(8,128)(2,1)}), bf16[32,1024,16]{1,2,0:T(8,128)(2,1)S(1)}, u32[]{:S(2)}, u32[]{:S(2)}) async-start(bf16[32,1024,16]{1,2,0:T(8,128)(2,1)} %broadcast_in_dim.37), calls=%async_computation.4 | async-start | bytes 2097152 | tf_op jit(solution)/shard_map/all_to_all | solution.py:36
  58.0 46.4 %copy-start.4 = (bf16[2,64,1024]{2,1,0:T(8,128)(2,1)S(1)}, bf16[2,64,1024]{2,1,0:T(8,128)(2,1)}, u32[]{:S(2)}) copy-start(bf16[2,64,1024]{2,1,0:T(8,128)(2,1)} %param.7) | copy-start | bytes 786436
  93.9 10.9 %copy-start.2 = (bf16[32,1024,16]{1,2,0:T(8,128)(2,1)}, bf16[32,1024,16]{1,2,0:T(8,128)(2,1)S(1)}, u32[]{:S(2)}) copy-start(bf16[32,1024,16]{1,2,0:T(8,128)(2,1)S(1)} %all-to-all-done.4) | copy-start | bytes 3145732
  95.2 39.7 %all-to-all-start = ((bf16[32,1024,16]{1,2,0:T(8,128)(2,1)}), bf16[32,1024,16]{1,2,0:T(8,128)(2,1)S(1)}, u32[]{:S(2)}, u32[]{:S(2)}) async-start(bf16[32,1024,16]{1,2,0:T(8,128)(2,1)} %broadcast_in_dim.33), calls=%async_computation | async-start | bytes 2097152 | tf_op jit(solution)/shard_map/all_to_all | solution.py:36
  134.8 1.7 copy-start.3
  136.5 56.5 %all-to-all-start.5 = ((bf16[32,64,512]{2,1,0:T(8,128)(2,1)}), bf16[32,64,512]{2,1,0:T(8,128)(2,1)S(1)}, u32[]{:S(2)}, u32[]{:S(2)}) async-start(bf16[32,64,512]{2,1,0:T(8,128)(2,1)} %stack.16), calls=%async_computation.5 | async-start | bytes 4194304 | tf_op jit(solution)/shard_map/all_to_all | solution.py:17
  193.0 2.0 copy-start.1
  194.9 56.4 %all-to-all-start.1 = ((bf16[32,64,512]{2,1,0:T(8,128)(2,1)}), bf16[32,64,512]{2,1,0:T(8,128)(2,1)S(1)}, u32[]{:S(2)}, u32[]{:S(2)}) async-start(bf16[32,64,512]{2,1,0:T(8,128)(2,1)} %stack.14), calls=%async_computation.1 | async-start | bytes 4194304 | tf_op jit(solution)/shard_map/all_to_all | solution.py:17
  251.4 20.0 %all-to-all-start.6 = ((f32[16,32,256]{2,1,0:T(8,128)}), f32[16,32,256]{2,1,0:T(8,128)}, u32[]{:S(2)}, u32[]{:S(2)}) async-start(f32[16,32,256]{2,1,0:T(8,128)} %fusion.4), calls=%async_computation.6 | async-start | bytes 1048576 | tf_op jit(solution)/shard_map/all_to_all | solution.py:57
  258.1 32.7 %copy-start.5 = (f32[2,32,256]{2,1,0:T(8,128)S(1)}, f32[2,32,256]{2,1,0:T(8,128)}, u32[]{:S(2)}) copy-start(f32[2,32,256]{2,1,0:T(8,128)} %param.9) | copy-start | bytes 196612
  258.1 32.7 %copy-start.6 = (f32[2,32,256]{2,1,0:T(8,128)S(1)}, f32[2,32,256]{2,1,0:T(8,128)}, u32[]{:S(2)}) copy-start(f32[2,32,256]{2,1,0:T(8,128)} %param.10) | copy-start | bytes 196612
  271.3 19.4 %all-to-all-start.2 = ((f32[16,32,256]{2,1,0:T(8,128)}), f32[16,32,256]{2,1,0:T(8,128)S(1)}, u32[]{:S(2)}, u32[]{:S(2)}) async-start(f32[16,32,256]{2,1,0:T(8,128)} %fusion.6), calls=%async_computation.2 | async-start | bytes 1048576 | tf_op jit(solution)/shard_map/all_to_all | solution.py:57
  305.6 13.4 %all-to-all-start.7 = ((bf16[16,32,256]{2,1,0:T(8,128)(2,1)}), bf16[16,32,256]{2,1,0:T(8,128)(2,1)S(1)}, u32[]{:S(2)}, u32[]{:S(2)}) async-start(bf16[16,32,256]{2,1,0:T(8,128)(2,1)} %broadcast_in_dim.39), calls=%async_computation.7 | async-start | bytes 524288 | tf_op jit(solution)/shard_map/all_to_all | solution.py:36
